TPU v7x, 32 devices: a whole 2x2x4 slice. The times are simulated.
32 devices in a mesh: dp: 8 (over y, x, core), seq: 4 (over z).
Axes of the slice: x: 2, y: 2, z: 4, core: 2. Of those that a mesh axis runs over, the one named last changes fastest.
Arguments:
- inputs: bfloat16 [16, 2048, 1024], P('dp', 'seq'), may hold values from -6 to 6
- cotangent: bfloat16 [16, 2048, 1024], P('dp', 'seq'), may hold values from -6 to 6
- segment_ids: int32 [16, 2048], P('dp'), may hold values from 0 to 21, as said below
- query_weight: bfloat16 [1024, 1024], P(('dp', 'seq')), may hold values from -0.1875 to 0.1875
- key_weight: bfloat16 [1024, 1024], P(('dp', 'seq')), may hold values from -0.1875 to 0.1875
- value_weight: bfloat16 [1024, 1024], P(('dp', 'seq')), may hold values from -0.1875 to 0.1875
- output_weight: bfloat16 [1024, 1024], P(('dp', 'seq')), may hold values from -0.1875 to 0.1875
- up_weight: bfloat16 [1024, 4096], P(('dp', 'seq')), may hold values from -0.1875 to 0.1875
- down_weight: bfloat16 [4096, 1024], P(('dp', 'seq')), may hold values from -0.09375 to 0.09375
- first_gain: float32 [1024], replicated, may hold values from 0.25 to 1.75
- first_shift: float32 [1024], replicated, may hold values from -1 to 1
- query_bias: float32 [1024], replicated, may hold values from -1 to 1
- value_bias: float32 [1024], replicated, may hold values from -1 to 1
- head_scale: float32 [16], replicated, may hold values from 0.3 to 3
- output_bias: float32 [1024], replicated, may hold values from -1 to 1
- post_gain: float32 [1024], replicated, may hold values from 0.25 to 1.75
- post_shift: float32 [1024], replicated, may hold values from -1 to 1
- second_gain: float32 [1024], replicated, may hold values from 0.25 to 1.75
- second_shift: float32 [1024], replicated, may hold values from -1 to 1
- up_bias: float32 [4096], replicated, may hold values from -1 to 1
- middle_gain: float32 [4096], replicated, may hold values from 0.25 to 1.75
- middle_shift: float32 [4096], replicated, may hold values from -1 to 1
- down_bias: float32 [1024], replicated, may hold values from -1 to 1
Outputs:
- layer_output: bfloat16 [16, 2048, 1024], P('dp', 'seq')
- input_grad: bfloat16 [16, 2048, 1024], P('dp', 'seq')
- query_weight_grad: float32 [1024, 1024], P(('dp', 'seq'))
- key_weight_grad: float32 [1024, 1024], P(('dp', 'seq'))
- value_weight_grad: float32 [1024, 1024], P(('dp', 'seq'))
- output_weight_grad: float32 [1024, 1024], P(('dp', 'seq'))
- up_weight_grad: float32 [1024, 4096], P(('dp', 'seq'))
- down_weight_grad: float32 [4096, 1024], P(('dp', 'seq'))
- first_gain_grad: float32 [1024], replicated
- first_shift_grad: float32 [1024], replicated
- query_bias_grad: float32 [1024], replicated
- value_bias_grad: float32 [1024], replicated
- head_scale_grad: float32 [16], replicated
- output_bias_grad: float32 [1024], replicated
- post_gain_grad: float32 [1024], replicated
- post_shift_grad: float32 [1024], replicated
- second_gain_grad: float32 [1024], replicated
- second_shift_grad: float32 [1024], replicated
- up_bias_grad: float32 [4096], replicated
- middle_gain_grad: float32 [4096], replicated
- middle_shift_grad: float32 [4096], replicated
- down_bias_grad: float32 [1024], replicated
Inputs may be any that keep to these rules, and one draw needn't show every extreme that they name: `segment_ids`: along each sequence the ids start at 0 and never fall; each document (a run of equal ids) has 60 to 800 positions, except the last of a sequence, which the sequence's end may cut short; in each sequence the first or the second document has exactly 800 positions; the last sequence reaches the largest id.
All inputs are finite; a program needn't handle non-finite values.
Results may differ from a plain program's by a relative error of at most 0.014.
Values may be sent and summed in bfloat16 or wider, within the bound.
A program may use at most 184 MiB of HBM per device.

v0:
```python
import jax
import jax.numpy as jnp
from jax import lax
from jax.sharding import PartitionSpec as P

EPSILON = 1e-05
MASKED = -1e30


def layer_norm(values, gain_vec, shift_vec):
    row_mean = jnp.mean(values, -1, keepdims=True)
    centred = values - row_mean
    spread = jnp.mean(centred * centred, -1, keepdims=True)
    return centred * lax.rsqrt(spread + EPSILON) * gain_vec + shift_vec


def exact_gelu(values):
    return jax.nn.gelu(values, approximate=False)


def matmul(left_side, right_side):
    return jnp.dot(left_side, right_side, preferred_element_type=jnp.float32)


def contract_rows(left_side, right_side):
    return lax.dot_general(
        left_side, right_side, (((0,), (0,)), ((), ())), preferred_element_type=jnp.float32
    )


def contract_last(left_side, right_side):
    return lax.dot_general(
        left_side, right_side, (((1,), (1,)), ((), ())), preferred_element_type=jnp.float32
    )


def split_heads(matrix, head_count):
    return matrix.reshape(matrix.shape[0], head_count, -1).transpose(1, 0, 2)


def join_heads(stacked):
    return stacked.transpose(1, 0, 2).reshape(stacked.shape[1], -1)


def head_scores(single_query_head, single_key_head, allowed, logit_scale_factor):
    score_matrix = contract_last(single_query_head, single_key_head) * logit_scale_factor
    return jnp.where(allowed, score_matrix, MASKED)


def local(
    inputs,
    cotangent,
    segment_ids,
    query_weight,
    key_weight,
    value_weight,
    output_weight,
    up_weight,
    down_weight,
    first_gain,
    first_shift,
    query_bias,
    value_bias,
    head_scale,
    output_bias,
    post_gain,
    post_shift,
    second_gain,
    second_shift,
    up_bias,
    middle_gain,
    middle_shift,
    down_bias,
):
    micro_count, row_count, model_width = inputs.shape
    hidden_width = up_bias.shape[0]
    head_count = head_scale.shape[0]
    logit_scale_factor = (model_width // head_count) ** (-0.5)
    seq_ranks = lax.axis_size("seq")
    rank_index = lax.axis_index("seq")
    length = row_count * seq_ranks
    query_place = rank_index * row_count + jnp.arange(row_count)
    causal = jnp.arange(length)[None, :] <= query_place[:, None]
    square = (model_width, model_width)
    matrix_sums = [
        jnp.zeros(square, jnp.float32),
        jnp.zeros(square, jnp.float32),
        jnp.zeros(square, jnp.float32),
        jnp.zeros(square, jnp.float32),
        jnp.zeros((model_width, hidden_width), jnp.float32),
        jnp.zeros((hidden_width, model_width), jnp.float32),
    ]
    vectors = (
        first_gain,
        first_shift,
        query_bias,
        value_bias,
        head_scale,
        output_bias,
        post_gain,
        post_shift,
        second_gain,
        second_shift,
        up_bias,
        middle_gain,
        middle_shift,
        down_bias,
    )
    vector_sums = [jnp.zeros_like(tensor) for tensor in vectors]
    outputs = []
    input_grads = []
    for micro_step in range(micro_count):
        tokens = inputs[micro_step].astype(jnp.float32)
        segment_row = segment_ids[micro_step]
        segment_query = lax.dynamic_slice_in_dim(segment_row, rank_index * row_count, row_count)
        attention_full = (
            lax.all_gather(query_weight, ("dp", "seq"), axis=0, tiled=True),
            lax.all_gather(key_weight, ("dp", "seq"), axis=0, tiled=True),
            lax.all_gather(value_weight, ("dp", "seq"), axis=0, tiled=True),
            lax.all_gather(output_weight, ("dp", "seq"), axis=0, tiled=True),
        )
        query_full, key_full, value_full, output_full = attention_full
        normed, first_back = jax.vjp(layer_norm, tokens, first_gain, first_shift)
        normed_low = normed.astype(jnp.bfloat16)
        query_low = (matmul(normed_low, query_full) + query_bias).astype(jnp.bfloat16)
        key_low = matmul(normed_low, key_full).astype(jnp.bfloat16)
        value_low = (matmul(normed_low, value_full) + value_bias).astype(jnp.bfloat16)
        key_all, value_all = (
            lax.all_gather(key_low, "seq", axis=0, tiled=True),
            lax.all_gather(value_low, "seq", axis=0, tiled=True),
        )
        allowed = causal & (segment_row[None, :] == segment_query[:, None])
        query_heads = split_heads(query_low, head_count)
        key_heads = split_heads(key_all, head_count)
        value_heads = split_heads(value_all, head_count)

        def attend(packed):
            single_query_head, single_key_head, single_value_head = packed
            score_matrix = head_scores(
                single_query_head, single_key_head, allowed, logit_scale_factor
            )
            largest = jnp.max(score_matrix, -1, keepdims=True)
            exponent = jnp.exp(score_matrix - largest)
            row_total = jnp.sum(exponent, -1, keepdims=True)
            weights_low = (exponent / row_total).astype(jnp.bfloat16)
            return (matmul(weights_low, single_value_head), (largest + jnp.log(row_total))[:, 0])

        attended, logsums = lax.map(attend, (query_heads, key_heads, value_heads))
        scaled_low = join_heads(attended * head_scale[:, None, None]).astype(jnp.bfloat16)
        branch = matmul(scaled_low, output_full) + output_bias
        posted, post_back = jax.vjp(layer_norm, branch, post_gain, post_shift)
        middle = tokens + posted
        feedforward_full = (
            lax.all_gather(up_weight, ("dp", "seq"), axis=0, tiled=True),
            lax.all_gather(down_weight, ("dp", "seq"), axis=0, tiled=True),
        )
        up_full, down_full = feedforward_full
        normed_two, second_back = jax.vjp(layer_norm, middle, second_gain, second_shift)
        second_low = normed_two.astype(jnp.bfloat16)
        upper_pre = matmul(second_low, up_full) + up_bias
        activated, gelu_back = jax.vjp(exact_gelu, upper_pre)
        mixed, middle_back = jax.vjp(layer_norm, activated, middle_gain, middle_shift)
        mixed_low = mixed.astype(jnp.bfloat16)
        output = middle + matmul(mixed_low, down_full) + down_bias
        outputs.append(output.astype(jnp.bfloat16))
        query_full, key_full, value_full, output_full = (
            lax.all_gather(query_weight, ("dp", "seq"), axis=0, tiled=True),
            lax.all_gather(key_weight, ("dp", "seq"), axis=0, tiled=True),
            lax.all_gather(value_weight, ("dp", "seq"), axis=0, tiled=True),
            lax.all_gather(output_weight, ("dp", "seq"), axis=0, tiled=True),
        )
        up_full, down_full = (
            lax.all_gather(up_weight, ("dp", "seq"), axis=0, tiled=True),
            lax.all_gather(down_weight, ("dp", "seq"), axis=0, tiled=True),
        )
        grad_low = cotangent[micro_step]
        grad_out = grad_low.astype(jnp.float32)
        grad_mixed = contract_last(grad_low, down_full)
        grad_activated, middle_gain_term, middle_shift_term = middle_back(grad_mixed)
        (grad_upper,) = gelu_back(grad_activated)
        upper_low = grad_upper.astype(jnp.bfloat16)
        grad_second = contract_last(upper_low, up_full)
        grad_middle_part, second_gain_term, second_shift_term = second_back(grad_second)
        grad_middle = grad_out + grad_middle_part
        grad_branch, post_gain_term, post_shift_term = post_back(grad_middle)
        branch_low = grad_branch.astype(jnp.bfloat16)
        grad_scaled = split_heads(contract_last(branch_low, output_full), head_count)
        head_term = jnp.sum(grad_scaled * attended, axis=(1, 2))
        grad_attended = (grad_scaled * head_scale[:, None, None]).astype(jnp.bfloat16)

        def attend_back(packed):
            single_query_head, single_key_head, single_value_head, grad_head, logsum = packed
            score_matrix = head_scores(
                single_query_head, single_key_head, allowed, logit_scale_factor
            )
            attention_probabilities = jnp.exp(score_matrix - logsum[:, None])
            weights_low = attention_probabilities.astype(jnp.bfloat16)
            grad_weights = contract_last(grad_head, single_value_head)
            grad_value = contract_rows(weights_low, grad_head)
            row_inner = jnp.sum(attention_probabilities * grad_weights, -1, keepdims=True)
            grad_scores = (attention_probabilities * (grad_weights - row_inner)).astype(
                jnp.bfloat16
            )
            grad_query = matmul(grad_scores, single_key_head) * logit_scale_factor
            grad_key = contract_rows(grad_scores, single_query_head) * logit_scale_factor
            return (grad_query, grad_key, grad_value)

        grad_queries, grad_keys, grad_values = lax.map(
            attend_back, (query_heads, key_heads, value_heads, grad_attended, logsums)
        )
        query_grad_low = join_heads(grad_queries).astype(jnp.bfloat16)
        key_sum, value_sum = (
            lax.psum_scatter(
                join_heads(grad_keys).astype(jnp.bfloat16), "seq", scatter_dimension=0, tiled=True
            ).astype(jnp.float32),
            lax.psum_scatter(
                join_heads(grad_values).astype(jnp.bfloat16), "seq", scatter_dimension=0, tiled=True
            ).astype(jnp.float32),
        )
        key_grad_low = key_sum.astype(jnp.bfloat16)
        value_grad_low = value_sum.astype(jnp.bfloat16)
        grad_normed = (
            contract_last(query_grad_low, query_full)
            + contract_last(key_grad_low, key_full)
            + contract_last(value_grad_low, value_full)
        )
        grad_tokens, first_gain_term, first_shift_term = first_back(grad_normed)
        input_grads.append((grad_middle + grad_tokens).astype(jnp.bfloat16))
        matrix_terms = (
            contract_rows(normed_low, query_grad_low),
            contract_rows(normed_low, key_grad_low),
            contract_rows(normed_low, value_grad_low),
            contract_rows(scaled_low, branch_low),
            contract_rows(second_low, upper_low),
            contract_rows(mixed_low, grad_low),
        )
        matrix_sums = [running + adding for running, adding in zip(matrix_sums, matrix_terms)]
        vector_terms = (
            first_gain_term,
            first_shift_term,
            jnp.sum(query_grad_low.astype(jnp.float32), 0),
            jnp.sum(value_grad_low.astype(jnp.float32), 0),
            head_term,
            jnp.sum(branch_low.astype(jnp.float32), 0),
            post_gain_term,
            post_shift_term,
            second_gain_term,
            second_shift_term,
            jnp.sum(upper_low.astype(jnp.float32), 0),
            middle_gain_term,
            middle_shift_term,
            jnp.sum(grad_out, 0),
        )
        vector_sums = [running + adding for running, adding in zip(vector_sums, vector_terms)]
    weight_parts = (
        lax.psum_scatter(matrix_sums[0], ("dp", "seq"), scatter_dimension=0, tiled=True),
        lax.psum_scatter(matrix_sums[1], ("dp", "seq"), scatter_dimension=0, tiled=True),
        lax.psum_scatter(matrix_sums[2], ("dp", "seq"), scatter_dimension=0, tiled=True),
        lax.psum_scatter(matrix_sums[3], ("dp", "seq"), scatter_dimension=0, tiled=True),
        lax.psum_scatter(matrix_sums[4], ("dp", "seq"), scatter_dimension=0, tiled=True),
        lax.psum_scatter(matrix_sums[5], ("dp", "seq"), scatter_dimension=0, tiled=True),
    )
    vector_parts = lax.psum(
        (
            vector_sums[0],
            vector_sums[1],
            vector_sums[2],
            vector_sums[3],
            vector_sums[4],
            vector_sums[5],
            vector_sums[6],
            vector_sums[7],
            vector_sums[8],
            vector_sums[9],
            vector_sums[10],
            vector_sums[11],
            vector_sums[12],
            vector_sums[13],
        ),
        ("dp", "seq"),
    )
    return (
        jnp.stack(outputs),
        jnp.stack(input_grads),
        weight_parts[0],
        weight_parts[1],
        weight_parts[2],
        weight_parts[3],
        weight_parts[4],
        weight_parts[5],
        vector_parts[0],
        vector_parts[1],
        vector_parts[2],
        vector_parts[3],
        vector_parts[4],
        vector_parts[5],
        vector_parts[6],
        vector_parts[7],
        vector_parts[8],
        vector_parts[9],
        vector_parts[10],
        vector_parts[11],
        vector_parts[12],
        vector_parts[13],
    )


def solution(mesh):
    in_specs = (
        P("dp", "seq", None),
        P("dp", "seq", None),
        P("dp", None),
        P(("dp", "seq"), None),
        P(("dp", "seq"), None),
        P(("dp", "seq"), None),
        P(("dp", "seq"), None),
        P(("dp", "seq"), None),
        P(("dp", "seq"), None),
        P(),
        P(),
        P(),
        P(),
        P(),
        P(),
        P(),
        P(),
        P(),
        P(),
        P(),
        P(),
        P(),
        P(),
    )
    out_specs = (
        P("dp", "seq", None),
        P("dp", "seq", None),
        P(("dp", "seq"), None),
        P(("dp", "seq"), None),
        P(("dp", "seq"), None),
        P(("dp", "seq"), None),
        P(("dp", "seq"), None),
        P(("dp", "seq"), None),
        P(),
        P(),
        P(),
        P(),
        P(),
        P(),
        P(),
        P(),
        P(),
        P(),
        P(),
        P(),
        P(),
        P(),
    )
    return jax.shard_map(local, mesh=mesh, in_specs=in_specs, out_specs=out_specs, check_vma=False)
```

profile of v0, /device:TPU:0, one launch (start us, length us, event | category | flops | bytes accessed | tf_op | source)
XLA Modules:
  0.0 2929.8 jit_solution(12358509383623044732)
XLA Ops:
  12.2 57.9 %all-gather.13.cloned.1.call-done = bf16[1024,1024]{1,0:T(8,128)(2,1)} async-done(((bf16[32,1024]{1,0:T(8,128)(2,1)}), bf16[1024,1024]{1,0:T(8,128)(2,1)}) %all-gather.13.cloned.1.call-update) | async-done | bytes 2097168 | tf_op jit(solution)/shard_map/all_gather | solution.py:118
  74.1 54.2 %all-gather.17.cloned.1.call-done = bf16[1024,1024]{1,0:T(8,128)(2,1)} async-done(((bf16[32,1024]{1,0:T(8,128)(2,1)}), bf16[1024,1024]{1,0:T(8,128)(2,1)}) %all-gather.17.cloned.1.call-update) | async-done | bytes 2097168 | tf_op jit(solution)/shard_map/all_gather | solution.py:119
  143.8 42.6 %all-gather.11.cloned.1.call-done = bf16[1024,1024]{1,0:T(8,128)(2,1)} async-done(((bf16[32,1024]{1,0:T(8,128)(2,1)}), bf16[1024,1024]{1,0:T(8,128)(2,1)}) %all-gather.11.cloned.1.call-update) | async-done | bytes 2097168 | tf_op jit(solution)/shard_map/all_gather | solution.py:117
  202.6 64.8 %all-gather.15.cloned.1.call-done = bf16[2048,1024]{1,0:T(8,128)(2,1)} async-done(((bf16[512,1024]{1,0:T(8,128)(2,1)}), bf16[2048,1024]{1,0:T(8,128)(2,1)}) %all-gather.15.cloned.1.call-update) | async-done | bytes 4194320 | tf_op jit(solution)/shard_map/all_gather | solution.py:129
  282.4 65.7 %all-gather.19.cloned.1.call-done = bf16[2048,1024]{1,0:T(8,128)(2,1)} async-done(((bf16[512,1024]{1,0:T(8,128)(2,1)}), bf16[2048,1024]{1,0:T(8,128)(2,1)}) %all-gather.19.cloned.1.call-update) | async-done | bytes 4194320 | tf_op jit(solution)/shard_map/all_gather | solution.py:130
  364.8 94.9 %while.56 = (s32[]{:T(128)}, f32[16,512,64]{1,2,0:T(8,128)}, f32[16,512]{1,0:T(8,128)S(1)}, bf16[16,512,64]{2,1,0:T(8,128)(2,1)}, bf16[16,2048,64]{2,1,0:T(8,128...) while((s32[]{:T(128)}, f32[16,512,64]{1,2,0:T(8,128)}, ...), condition=%wide.region_5.6_spmd.clone, body=%wide.region_2.5_spmd.clone.sunk | while | flops 279969280 | bytes 13928569 | solution.py:148
  474.7 34.9 %all-gather.29.cloned.1.call-done = bf16[2048,1024]{1,0:T(8,128)(2,1)} async-done(((bf16[512,1024]{1,0:T(8,128)(2,1)}), bf16[2048,1024]{1,0:T(8,128)(2,1)}) %all-gather.29.cloned.1.call-update) | async-done | bytes 4194320 | tf_op jit(solution)/shard_map/all_gather | solution.py:130
  526.2 95.4 %while.57 = (s32[]{:T(128)}, f32[16,512,64]{1,2,0:T(8,128)}, f32[16,512]{1,0:T(8,128)S(1)}, bf16[16,512,64]{2,1,0:T(8,128)(2,1)}, bf16[16,2048,64]{2,1,0:T(8,128...) while((s32[]{:T(128)}, f32[16,512,64]{1,2,0:T(8,128)}, ...), condition=%wide.region_17.18_spmd.clone, body=%wide.region_14.17_spmd.clone.sunk | while | flops 279969280 | bytes 13928569 | solution.py:148
  654.2 48.7 %fusion.197 = (f32[512]{0:T(512)S(1)}, f32[512,4096]{1,0:T(8,128)}, f32[512,4096]{1,0:T(8,128)}, f32[512]{0:T(512)S(1)}, f32[512,4096]{1,0:T(8,128)}, /*index=5*/f32[512,4096]{1,0:T(8,128)}, f32[512,4096]{1,0:T(8,128)}) fusion(f32[4096]{0:T(1024)S(1)} %copy-done.107, f32[512,4096]{1,0:T(8,128)S(1)} %fusion.178, ...), kind=kOutput, calls=%fused_computation.343 | convolution fusion | flops 4574411776 | bytes 60850176 | tf_op jit(solution)/shard_map/dot_general | solution.py:22
  703.0 21.8 all-gather.25.cloned.1.call-done
  724.8 11.6 fusion.146
  736.4 17.3 multiply_reduce_fusion.5
  753.8 15.1 multiply_reduce_fusion.2
  768.9 24.0 convert_reduce_fusion
  803.2 10.6 multiply_reduce_fusion.8
  834.2 178.0 %while.59 = (s32[]{:T(128)}, bf16[16,512,64]{1,2,0:T(8,128)(2,1)S(1)}, bf16[16,2048,64]{1,2,0:T(8,128)(2,1)}, bf16[16,2048,64]{1,2,0:T(8,128)(2,1)}, bf16[16,512...) while((s32[]{:T(128)}, ...), condition=%wide.region_45.46_spmd.clone, body=%wide.region_43.45_spmd.clone.sunk | while | flops 683834880 | bytes 34630792 | solution.py:208
  1017.3 178.0 %while.58 = (s32[]{:T(128)}, bf16[16,512,64]{1,2,0:T(8,128)(2,1)S(1)}, bf16[16,2048,64]{1,2,0:T(8,128)(2,1)}, bf16[16,2048,64]{1,2,0:T(8,128)(2,1)}, bf16[16,512...) while((s32[]{:T(128)}, ...), condition=%wide.region_32.33_spmd.clone, body=%wide.region_30.32_spmd.clone.sunk | while | flops 683834880 | bytes 34630792 | solution.py:208
  1233.7 37.2 %reduce-scatter.11.cloned.1.call-done = bf16[512,1024]{0,1:T(8,128)(2,1)} async-done(((bf16[2048,1024]{0,1:T(8,128)(2,1)}), bf16[512,1024]{0,1:T(8,128)(2,1)}) %reduce-scatter.11.cloned.1.call-update) | async-done | bytes 1048592 | tf_op jit(solution)/shard_map/reduce_scatter | solution.py:213
  1275.5 75.0 %reduce-scatter.17.cloned.1.call-done = bf16[512,1024]{0,1:T(8,128)(2,1)} async-done(((bf16[2048,1024]{0,1:T(8,128)(2,1)}), bf16[512,1024]{0,1:T(8,128)(2,1)}) %reduce-scatter.17.cloned.1.call-update) | async-done | bytes 1048592 | tf_op jit(solution)/shard_map/reduce_scatter | solution.py:216
  1356.3 73.7 %reduce-scatter.13.cloned.1.call-done = bf16[512,1024]{0,1:T(8,128)(2,1)} async-done(((bf16[2048,1024]{0,1:T(8,128)(2,1)}), bf16[512,1024]{0,1:T(8,128)(2,1)}) %reduce-scatter.13.cloned.1.call-update) | async-done | bytes 1048592 | tf_op jit(solution)/shard_map/reduce_scatter | solution.py:216
  1454.4 13.5 fusion.176
  1467.9 11.9 convolution_add_fusion
  1480.5 14.5 fusion.148
  1494.9 15.0 convolution_add_fusion.1
  1510.6 11.1 fusion.137
  1538.3 43.6 %reduce-scatter.19.cloned.1.call-done = f32[32,1024]{1,0:T(8,128)} async-done(((f32[1024,1024]{1,0:T(8,128)}), f32[32,1024]{1,0:T(8,128)}) %reduce-scatter.19.cloned.1.call-update) | async-done | bytes 131088 | tf_op jit(solution)/shard_map/reduce_scatter | solution.py:256
  1581.9 151.3 %reduce-scatter.25.cloned.1.call-done = f32[32,1024]{1,0:T(8,128)} async-done(((f32[1024,1024]{1,0:T(8,128)}), f32[32,1024]{1,0:T(8,128)}) %reduce-scatter.25.cloned.1.call-update) | async-done | bytes 131088 | tf_op jit(solution)/shard_map/reduce_scatter | solution.py:259
  1733.2 140.7 %all-reduce.3.cloned.1.call-done = (f32[1024]{0:T(1024)}, f32[1024]{0:T(1024)}, f32[1024]{0:T(1024)}, f32[1024]{0:T(1024)}, f32[16]{0:T(128)}, /*index=5*/f32[10...) async-done(((f32[1024]{0:T(1024)}, f32[1024]{0:T(1024)}, ...) | async-done | bytes 90192 | tf_op jit(solution)/shard_map/psum | solution.py:263
  1873.9 153.3 %reduce-scatter.21.cloned.1.call-done = f32[32,1024]{1,0:T(8,128)} async-done(((f32[1024,1024]{1,0:T(8,128)}), f32[32,1024]{1,0:T(8,128)}) %reduce-scatter.21.cloned.1.call-update) | async-done | bytes 131088 | tf_op jit(solution)/shard_map/reduce_scatter | solution.py:257
  2027.2 150.5 %reduce-scatter.23.cloned.1.call-done = f32[32,1024]{1,0:T(8,128)} async-done(((f32[1024,1024]{1,0:T(8,128)}), f32[32,1024]{1,0:T(8,128)}) %reduce-scatter.23.cloned.1.call-update) | async-done | bytes 131088 | tf_op jit(solution)/shard_map/reduce_scatter | solution.py:258
  2177.7 362.3 %reduce-scatter.27.cloned.1.call-done = f32[32,4096]{1,0:T(8,128)} async-done(((f32[1024,4096]{1,0:T(8,128)}), f32[32,4096]{1,0:T(8,128)}) %reduce-scatter.27.cloned.1.call-update) | async-done | bytes 524304 | tf_op jit(solution)/shard_map/reduce_scatter | solution.py:260
  2540.0 364.8 %reduce-scatter.29.cloned.1.call-done = f32[128,1024]{1,0:T(8,128)} async-done(((f32[4096,1024]{1,0:T(8,128)}), f32[128,1024]{1,0:T(8,128)}) %reduce-scatter.29.cloned.1.call-update) | async-done | bytes 524304 | tf_op jit(solution)/shard_map/reduce_scatter | solution.py:261
  (832 shorter events, 824.1 us)
Async XLA Ops:
  7.2 62.9 %all-gather.13.cloned.1.call-start = ((), (), s32[]{:S(2)}) async-start(), calls=%async_computation.11 | async-start | bytes 2162688 | tf_op jit(solution)/shard_map/all_gather | solution.py:118
  7.9 120.3 %all-gather.17.cloned.1.call-start = ((), (), s32[]{:S(2)}) async-start(), calls=%async_computation.13 | async-start | bytes 2162688 | tf_op jit(solution)/shard_map/all_gather | solution.py:119
  8.7 177.7 %all-gather.11.cloned.1.call-start = ((), (), s32[]{:S(2)}) async-start(), calls=%async_computation.10 | async-start | bytes 2162688 | tf_op jit(solution)/shard_map/all_gather | solution.py:117
  9.4 258.0 %all-gather.15.cloned.1.call-start = ((), (), s32[]{:S(2)}) async-start(), calls=%async_computation.12 | async-start | bytes 5242880 | tf_op jit(solution)/shard_map/all_gather | solution.py:129
  11.4 175.0 %copy-start.81 = (f32[512]{0:T(512)}, f32[512]{0:T(512)S(1)}, u32[]{:S(2)}) copy-start(f32[512]{0:T(512)S(1)} %get-tuple-element.589) | copy-start | bytes 6148
  11.4 183.9 %copy-start.53 = (f32[512]{0:T(512)}, f32[512]{0:T(512)S(1)}, u32[]{:S(2)}) copy-start(f32[512]{0:T(512)S(1)} %get-tuple-element.588) | copy-start | bytes 6148
  12.1 120.1 %copy-start.97 = (f32[512]{0:T(512)}, f32[512]{0:T(512)S(1)}, u32[]{:S(2)}) copy-start(f32[512]{0:T(512)S(1)} %get-tuple-element.397) | copy-start | bytes 6148
  12.1 174.3 %copy-start.89 = (f32[512]{0:T(512)}, f32[512]{0:T(512)S(1)}, u32[]{:S(2)}) copy-start(f32[512]{0:T(512)S(1)} %fusion.166) | copy-start | bytes 6148
  12.2 116.1 %copy-start.129 = (f32[1024]{0:T(1024)S(1)}, f32[1024]{0:T(1024)}, u32[]{:S(2)}) copy-start(f32[1024]{0:T(1024)} %param.43) | copy-start | bytes 12292
  74.0 274.1 %all-gather.19.cloned.1.call-start = ((), (), s32[]{:S(2)}) async-start(), calls=%async_computation.14 | async-start | bytes 5242880 | tf_op jit(solution)/shard_map/all_gather | solution.py:130
  132.1 327.6 %all-gather.27.cloned.1.call-start = ((), (), s32[]{:S(2)}) async-start(), calls=%async_computation.18 | async-start | bytes 5242880 | tf_op jit(solution)/shard_map/all_gather | solution.py:129
  136.2 373.5 %all-gather.29.cloned.1.call-start = ((), (), s32[]{:S(2)}) async-start(), calls=%async_computation.19 | async-start | bytes 5242880 | tf_op jit(solution)/shard_map/all_gather | solution.py:130
  140.2 486.0 %all-gather.21.cloned.1.call-start = ((), (), s32[]{:S(2)}) async-start(), calls=%async_computation.15 | async-start | bytes 2162688 | tf_op jit(solution)/shard_map/all_gather | solution.py:120
  140.9 505.4 %all-gather.23.cloned.1.call-start = ((), (), s32[]{:S(2)}) async-start(), calls=%async_computation.16 | async-start | bytes 8650752 | tf_op jit(solution)/shard_map/all_gather | solution.py:154
  141.7 583.1 %all-gather.25.cloned.1.call-start = ((), (), s32[]{:S(2)}) async-start(), calls=%async_computation.17 | async-start | bytes 8650752 | tf_op jit(solution)/shard_map/all_gather | solution.py:155
  142.3 1086.9 %reduce-scatter.15.cloned.1.call-start = ((), (), s32[]{:S(2)}) async-start(), calls=%async_computation.22 | async-start | bytes 5242880 | tf_op jit(solution)/shard_map/reduce_scatter | solution.py:213
  526.2 96.0 %copy-start.120 = (f32[16]{0:T(128)S(1)}, f32[16]{0:T(128)}, u32[]{:S(2)}) copy-start(f32[16]{0:T(128)} %param.44) | copy-start | bytes 196
  634.5 179.4 %copy-start.95 = (f32[512]{0:T(512)}, f32[512]{0:T(512)S(1)}, u32[]{:S(2)}) copy-start(f32[512]{0:T(512)S(1)} %broadcast_multiply_fusion.5) | copy-start | bytes 6148
  636.0 177.8 %copy-start.115 = (f32[512]{0:T(512)}, f32[512]{0:T(512)S(1)}, u32[]{:S(2)}) copy-start(f32[512]{0:T(512)S(1)} %fusion.168) | copy-start | bytes 6148
  702.9 65.9 %copy-start.91 = (f32[512]{0:T(512)}, f32[512]{0:T(512)S(1)}, u32[]{:S(2)}) copy-start(f32[512]{0:T(512)S(1)} %broadcast_multiply_fusion.1) | copy-start | bytes 6148
  1012.2 258.7 %reduce-scatter.11.cloned.1.call-start = ((), (), s32[]{:S(2)}) async-start(), calls=%async_computation.20 | async-start | bytes 5242880 | tf_op jit(solution)/shard_map/reduce_scatter | solution.py:213
  1196.3 154.2 %reduce-scatter.17.cloned.1.call-start = ((), (), s32[]{:S(2)}) async-start(), calls=%async_computation.23 | async-start | bytes 5242880 | tf_op jit(solution)/shard_map/reduce_scatter | solution.py:216
  1197.0 233.0 %reduce-scatter.13.cloned.1.call-start = ((), (), s32[]{:S(2)}) async-start(), calls=%async_computation.21 | async-start | bytes 5242880 | tf_op jit(solution)/shard_map/reduce_scatter | solution.py:216
  1197.6 384.3 %reduce-scatter.19.cloned.1.call-start = ((), (), s32[]{:S(2)}) async-start(), calls=%async_computation.24 | async-start | bytes 4325376 | tf_op jit(solution)/shard_map/reduce_scatter | solution.py:256
  1205.0 528.2 %reduce-scatter.25.cloned.1.call-start = ((), (), s32[]{:S(2)}) async-start(), calls=%async_computation.27 | async-start | bytes 4325376 | tf_op jit(solution)/shard_map/reduce_scatter | solution.py:259
  1211.7 662.2 %all-reduce.3.cloned.1.call-start = ((), (), s32[]{:S(2)}) async-start(), calls=%async_computation.30 | async-start | bytes 181248 | tf_op jit(solution)/shard_map/psum | solution.py:263
  1356.3 79.8 %copy-start.100 = (f32[512]{0:T(512)S(1)}, f32[512]{0:T(512)}, u32[]{:S(2)}) copy-start(f32[512]{0:T(512)} %copy-done.99) | copy-start | bytes 6148
  1356.3 79.8 %copy-start.98 = (f32[512]{0:T(512)S(1)}, f32[512]{0:T(512)}, u32[]{:S(2)}) copy-start(f32[512]{0:T(512)} %copy-done.97) | copy-start | bytes 6148
  1440.7 586.5 %reduce-scatter.21.cloned.1.call-start = ((), (), s32[]{:S(2)}) async-start(), calls=%async_computation.25 | async-start | bytes 4325376 | tf_op jit(solution)/shard_map/reduce_scatter | solution.py:257
  1447.3 730.4 %reduce-scatter.23.cloned.1.call-start = ((), (), s32[]{:S(2)}) async-start(), calls=%async_computation.26 | async-start | bytes 4325376 | tf_op jit(solution)/shard_map/reduce_scatter | solution.py:258
  1453.7 1086.3 %reduce-scatter.27.cloned.1.call-start = ((), (), s32[]{:S(2)}) async-start(), calls=%async_computation.28 | async-start | bytes 17301504 | tf_op jit(solution)/shard_map/reduce_scatter | solution.py:260
  1479.8 1425.1 %reduce-scatter.29.cloned.1.call-start = ((), (), s32[]{:S(2)}) async-start(), calls=%async_computation.29 | async-start | bytes 17301504 | tf_op jit(solution)/shard_map/reduce_scatter | solution.py:261
  (123 other events, 1129.5 us)
Sparse Core Ops, SparseCore 0:
  10.9 59.0 all-gather.12
  73.0 55.1 all-gather.16
  131.2 55.1 all-gather.10
  187.8 79.5 all-gather.14
  268.9 79.2 all-gather.18
  349.5 79.2 all-gather.26
  430.4 79.2 all-gather.28
  512.5 54.8 all-gather.20
  570.4 75.9 all-gather.22
  649.1 75.6 all-gather.24
  1012.4 75.4 reduce-scatter.14
  1195.5 75.4 reduce-scatter.10
  1273.2 77.2 reduce-scatter.16
  1352.7 77.2 reduce-scatter.12
  1432.7 149.1 reduce-scatter.18
  1584.6 148.5 reduce-scatter.24
  1740.6 133.1 all-reduce.2
  1876.6 150.5 reduce-scatter.20
  2030.0 147.6 reduce-scatter.22
  2180.4 359.5 reduce-scatter.26
  2542.9 361.9 reduce-scatter.28
where the time goes:
time: 2950 us; the launch traced here: 2930 us
  waiting for transfers between devices  1910 us (65%)
  matrix products  750 us (25%)
  local copies, waits for them, and re-layouts  137 us (5%)
  other arithmetic  113 us (4%)
    reduce_scatter x1, waiting for transfers between devices, local(): lax.psum_scatter(matrix_sums[5], ('dp', 'seq'), scatter_dimension=0, tile...  365 us
    reduce_scatter x1, waiting for transfers between devices, local(): lax.psum_scatter(matrix_sums[4], ('dp', 'seq'), scatter_dimension=0, tile...  362 us
    dot_general x108, matrix products, contract_last(): lax.dot_general(left_side, right_side, (((1,), (1,)), ((), ())), preferre...  309 us
    dot_general x76, matrix products, matmul(): return jnp.dot(left_side, right_side, preferred_element_type=jnp.float32)  254 us
    dot_general x76, matrix products, contract_rows(): lax.dot_general(left_side, right_side, (((0,), (0,)), ((), ())), preferre...  187 us
    reduce_scatter x1, waiting for transfers between devices, local(): lax.psum_scatter(matrix_sums[1], ('dp', 'seq'), scatter_dimension=0, tile...  153 us
    reduce_scatter x1, waiting for transfers between devices, local(): lax.psum_scatter(matrix_sums[3], ('dp', 'seq'), scatter_dimension=0, tile...  151 us
    reduce_scatter x1, waiting for transfers between devices, local(): lax.psum_scatter(matrix_sums[2], ('dp', 'seq'), scatter_dimension=0, tile...  151 us
  transfers between devices with their start and end apart: 21, of which 18 were waited for; matrix products, arithmetic and copies ran while one was open for 23% of the time, Pallas kernels for 0%

commit v1 on v0

--- a/solution.py
+++ b/solution.py
@@ -5,6 +5,18 @@
 
 EPSILON = 1e-05
 MASKED = -1e30
+
+
+def gather_by_bits(shard, axis, dim):
+    ways, here, hop = (lax.axis_size(axis), lax.axis_index(axis), shard.shape[dim])
+    line, have = (shard, 1)
+    while have < ways:
+        line = jnp.concatenate(
+            [line, lax.ppermute(line, axis, [(d, (d - have) % ways) for d in range(ways)])],
+            axis=dim,
+        )
+        have = 2 * have
+    return jnp.roll(line, here * hop, axis=dim)
 
 
 def layer_norm(values, gain_vec, shift_vec):
@@ -127,7 +139,7 @@
         value_low = (matmul(normed_low, value_full) + value_bias).astype(jnp.bfloat16)
         key_all, value_all = (
             lax.all_gather(key_low, "seq", axis=0, tiled=True),
-            lax.all_gather(value_low, "seq", axis=0, tiled=True),
+            gather_by_bits(value_low, "seq", 0),
         )
         allowed = causal & (segment_row[None, :] == segment_query[:, None])
         query_heads = split_heads(query_low, head_count)

time: 2950 us -> 2980 us (1.010)
    all_gather x1, waiting for transfers between devices: 42.6 us -> 200 us  [local(): lax.all_gather(query_weight, ('dp', 'seq'), axis=0, tiled=True)]
    all_gather x2 -> x0, waiting for transfers between devices: 101 us -> none  [local(): lax.all_gather(value_low, 'seq', axis=0, tiled=True)]
    all_gather x2, waiting for transfers between devices: 64.8 us -> 12.2 us  [local(): lax.all_gather(key_low, 'seq', axis=0, tiled=True)]
    ppermute x0 -> x4, waiting for transfers between devices: none -> 41.4 us  [gather_by_bits(): lax.ppermute(line, axis, [(d, (d - have) % ways) for d in range(ways)])]
    unnamed x289 -> x299, local copies, waits for them, and re-layouts: 69 us -> 68.8 us
  transfers between devices with their start and end apart: 21 -> 23, of which waited for: 18 -> 17; matrix products, arithmetic and copies ran while one was open for 23% -> 24% of each run, Pallas kernels for 0% -> 0%
where the time goes in v1:
time: 2980 us; the launch traced here: 2970 us
  waiting for transfers between devices  1920 us (64%)
  matrix products  746 us (25%)
  other arithmetic  142 us (5%)
  local copies, waits for them, and re-layouts  136 us (5%)
    reduce_scatter x1, waiting for transfers between devices, local(): lax.psum_scatter(matrix_sums[5], ('dp', 'seq'), scatter_dimension=0, tile...  365 us
    reduce_scatter x1, waiting for transfers between devices, local(): lax.psum_scatter(matrix_sums[4], ('dp', 'seq'), scatter_dimension=0, tile...  362 us
    dot_general x108, matrix products, contract_last(): lax.dot_general(left_side, right_side, (((1,), (1,)), ((), ())), preferre...  309 us
    dot_general x76, matrix products, matmul(): return jnp.dot(left_side, right_side, preferred_element_type=jnp.float32)  250 us
    all_gather x1, waiting for transfers between devices, local(): lax.all_gather(query_weight, ('dp', 'seq'), axis=0, tiled=True)  200 us
    dot_general x76, matrix products, contract_rows(): lax.dot_general(left_side, right_side, (((0,), (0,)), ((), ())), preferre...  187 us
    reduce_scatter x1, waiting for transfers between devices, local(): lax.psum_scatter(matrix_sums[1], ('dp', 'seq'), scatter_dimension=0, tile...  153 us
    reduce_scatter x1, waiting for transfers between devices, local(): lax.psum_scatter(matrix_sums[3], ('dp', 'seq'), scatter_dimension=0, tile...  151 us
  transfers between devices with their start and end apart: 23, of which 17 were waited for; matrix products, arithmetic and copies ran while one was open for 24% of the time, Pallas kernels for 0%

profile of v1, /device:TPU:0, one launch (start us, length us, event | category | flops | bytes accessed | tf_op | source)
XLA Modules:
  0.0 2966.1 jit_solution(14889374191115359948)
XLA Ops:
  12.2 57.9 %all-gather.11.cloned.1.call-done = bf16[1024,1024]{1,0:T(8,128)(2,1)} async-done(((bf16[32,1024]{1,0:T(8,128)(2,1)}), bf16[1024,1024]{1,0:T(8,128)(2,1)}) %all-gather.11.cloned.1.call-update) | async-done | bytes 2097168 | tf_op jit(solution)/shard_map/all_gather | solution.py:130
  79.3 48.9 %all-gather.15.cloned.1.call-done = bf16[1024,1024]{1,0:T(8,128)(2,1)} async-done(((bf16[32,1024]{1,0:T(8,128)(2,1)}), bf16[1024,1024]{1,0:T(8,128)(2,1)}) %all-gather.15.cloned.1.call-update) | async-done | bytes 2097168 | tf_op jit(solution)/shard_map/all_gather | solution.py:131
  134.9 23.8 collective-permute-done
  163.5 17.6 collective-permute-done.2
  184.8 199.9 %all-gather.9.cloned.1.call-done = bf16[1024,1024]{1,0:T(8,128)(2,1)} async-done(((bf16[32,1024]{1,0:T(8,128)(2,1)}), bf16[1024,1024]{1,0:T(8,128)(2,1)}) %all-gather.9.cloned.1.call-update) | async-done | bytes 2097168 | tf_op jit(solution)/shard_map/all_gather | solution.py:129
  399.2 10.9 fusion.107
  425.1 13.6 fusion.102
  453.5 12.2 all-gather.13.cloned.1.call-done
  482.3 94.8 %while.56 = (s32[]{:T(128)}, f32[16,512,64]{1,2,0:T(8,128)}, f32[16,512]{1,0:T(8,128)S(1)}, bf16[16,512,64]{2,1,0:T(8,128)(2,1)}, bf16[16,2048,64]{2,1,0:T(8,128...) while((s32[]{:T(128)}, f32[16,512,64]{1,2,0:T(8,128)}, ...), condition=%wide.region_5.7_spmd.clone, body=%wide.region_2.6_spmd.clone.sunk | while | flops 279969280 | bytes 13928569 | solution.py:160
  593.6 95.5 %while.57 = (s32[]{:T(128)}, f32[16,512,64]{1,2,0:T(8,128)}, f32[16,512]{1,0:T(8,128)S(1)}, bf16[16,512,64]{2,1,0:T(8,128)(2,1)}, bf16[16,2048,64]{2,1,0:T(8,128...) while((s32[]{:T(128)}, f32[16,512,64]{1,2,0:T(8,128)}, ...), condition=%wide.region_17.19_spmd.clone, body=%wide.region_14.18_spmd.clone.sunk | while | flops 279969280 | bytes 13928569 | solution.py:160
  711.5 48.5 %fusion.207 = (f32[512]{0:T(512)S(1)}, f32[512,4096]{1,0:T(8,128)}, f32[512,4096]{1,0:T(8,128)}, f32[512]{0:T(512)S(1)}, f32[512,4096]{1,0:T(8,128)}, /*index=5*/f32[512,4096]{1,0:T(8,128)}, f32[512,4096]{1,0:T(8,128)}) fusion(f32[4096]{0:T(1024)S(1)} %copy-done.112, f32[512,4096]{1,0:T(8,128)S(1)} %fusion.188, ...), kind=kOutput, calls=%fused_computation.367 | convolution fusion | flops 4574411776 | bytes 60850176 | tf_op jit(solution)/shard_map/dot_general | solution.py:34
  761.8 11.6 fusion.156
  773.3 17.3 multiply_reduce_fusion.5
  790.7 15.1 multiply_reduce_fusion.2
  805.8 24.0 convert_reduce_fusion
  871.1 177.9 %while.59 = (s32[]{:T(128)}, bf16[16,512,64]{1,2,0:T(8,128)(2,1)S(1)}, bf16[16,2048,64]{1,2,0:T(8,128)(2,1)}, bf16[16,2048,64]{1,2,0:T(8,128)(2,1)}, bf16[16,512...) while((s32[]{:T(128)}, ...), condition=%wide.region_45.47_spmd.clone, body=%wide.region_43.46_spmd.clone.sunk | while | flops 683834880 | bytes 34630792 | solution.py:220
  1054.1 177.8 %while.58 = (s32[]{:T(128)}, bf16[16,512,64]{1,2,0:T(8,128)(2,1)S(1)}, bf16[16,2048,64]{1,2,0:T(8,128)(2,1)}, bf16[16,2048,64]{1,2,0:T(8,128)(2,1)}, bf16[16,512...) while((s32[]{:T(128)}, ...), condition=%wide.region_32.34_spmd.clone, body=%wide.region_30.33_spmd.clone.sunk | while | flops 683834880 | bytes 34630792 | solution.py:220
  1270.3 37.2 %reduce-scatter.11.cloned.1.call-done = bf16[512,1024]{0,1:T(8,128)(2,1)} async-done(((bf16[2048,1024]{0,1:T(8,128)(2,1)}), bf16[512,1024]{0,1:T(8,128)(2,1)}) %reduce-scatter.11.cloned.1.call-update) | async-done | bytes 1048592 | tf_op jit(solution)/shard_map/reduce_scatter | solution.py:225
  1312.0 75.1 %reduce-scatter.17.cloned.1.call-done = bf16[512,1024]{0,1:T(8,128)(2,1)} async-done(((bf16[2048,1024]{0,1:T(8,128)(2,1)}), bf16[512,1024]{0,1:T(8,128)(2,1)}) %reduce-scatter.17.cloned.1.call-update) | async-done | bytes 1048592 | tf_op jit(solution)/shard_map/reduce_scatter | solution.py:228
  1392.9 73.7 %reduce-scatter.13.cloned.1.call-done = bf16[512,1024]{0,1:T(8,128)(2,1)} async-done(((bf16[2048,1024]{0,1:T(8,128)(2,1)}), bf16[512,1024]{0,1:T(8,128)(2,1)}) %reduce-scatter.13.cloned.1.call-update) | async-done | bytes 1048592 | tf_op jit(solution)/shard_map/reduce_scatter | solution.py:228
  1491.0 13.5 fusion.186
  1504.4 11.8 convolution_add_fusion
  1516.9 14.5 fusion.158
  1531.4 14.9 convolution_add_fusion.1
  1547.1 11.1 fusion.147
  1574.8 44.2 %reduce-scatter.19.cloned.1.call-done = f32[32,1024]{1,0:T(8,128)} async-done(((f32[1024,1024]{1,0:T(8,128)}), f32[32,1024]{1,0:T(8,128)}) %reduce-scatter.19.cloned.1.call-update) | async-done | bytes 131088 | tf_op jit(solution)/shard_map/reduce_scatter | solution.py:268
  1619.1 150.8 %reduce-scatter.25.cloned.1.call-done = f32[32,1024]{1,0:T(8,128)} async-done(((f32[1024,1024]{1,0:T(8,128)}), f32[32,1024]{1,0:T(8,128)}) %reduce-scatter.25.cloned.1.call-update) | async-done | bytes 131088 | tf_op jit(solution)/shard_map/reduce_scatter | solution.py:271
  1769.9 141.3 %all-reduce.3.cloned.1.call-done = (f32[1024]{0:T(1024)}, f32[1024]{0:T(1024)}, f32[1024]{0:T(1024)}, f32[1024]{0:T(1024)}, f32[16]{0:T(128)}, /*index=5*/f32[10...) async-done(((f32[1024]{0:T(1024)}, f32[1024]{0:T(1024)}, ...) | async-done | bytes 90192 | tf_op jit(solution)/shard_map/psum | solution.py:275
  1911.2 153.1 %reduce-scatter.21.cloned.1.call-done = f32[32,1024]{1,0:T(8,128)} async-done(((f32[1024,1024]{1,0:T(8,128)}), f32[32,1024]{1,0:T(8,128)}) %reduce-scatter.21.cloned.1.call-update) | async-done | bytes 131088 | tf_op jit(solution)/shard_map/reduce_scatter | solution.py:269
  2064.2 150.3 %reduce-scatter.23.cloned.1.call-done = f32[32,1024]{1,0:T(8,128)} async-done(((f32[1024,1024]{1,0:T(8,128)}), f32[32,1024]{1,0:T(8,128)}) %reduce-scatter.23.cloned.1.call-update) | async-done | bytes 131088 | tf_op jit(solution)/shard_map/reduce_scatter | solution.py:270
  2214.6 362.2 %reduce-scatter.27.cloned.1.call-done = f32[32,4096]{1,0:T(8,128)} async-done(((f32[1024,4096]{1,0:T(8,128)}), f32[32,4096]{1,0:T(8,128)}) %reduce-scatter.27.cloned.1.call-update) | async-done | bytes 524304 | tf_op jit(solution)/shard_map/reduce_scatter | solution.py:272
  2576.8 364.8 %reduce-scatter.29.cloned.1.call-done = f32[128,1024]{1,0:T(8,128)} async-done(((f32[4096,1024]{1,0:T(8,128)}), f32[128,1024]{1,0:T(8,128)}) %reduce-scatter.29.cloned.1.call-update) | async-done | bytes 524304 | tf_op jit(solution)/shard_map/reduce_scatter | solution.py:273
  (848 shorter events, 829.0 us)
Async XLA Ops:
  7.2 62.9 %all-gather.11.cloned.1.call-start = ((), (), s32[]{:S(2)}) async-start(), calls=%async_computation.11 | async-start | bytes 2162688 | tf_op jit(solution)/shard_map/all_gather | solution.py:130
  7.9 120.3 %all-gather.15.cloned.1.call-start = ((), (), s32[]{:S(2)}) async-start(), calls=%async_computation.13 | async-start | bytes 2162688 | tf_op jit(solution)/shard_map/all_gather | solution.py:131
  8.7 376.0 %all-gather.9.cloned.1.call-start = ((), (), s32[]{:S(2)}) async-start(), calls=%async_computation.10 | async-start | bytes 2162688 | tf_op jit(solution)/shard_map/all_gather | solution.py:129
  9.4 456.3 %all-gather.13.cloned.1.call-start = ((), (), s32[]{:S(2)}) async-start(), calls=%async_computation.12 | async-start | bytes 5242880 | tf_op jit(solution)/shard_map/all_gather | solution.py:141
  11.4 373.3 %copy-start.86 = (f32[512]{0:T(512)}, f32[512]{0:T(512)S(1)}, u32[]{:S(2)}) copy-start(f32[512]{0:T(512)S(1)} %get-tuple-element.590) | copy-start | bytes 6148
  11.4 380.4 %copy-start.58 = (f32[512]{0:T(512)}, f32[512]{0:T(512)S(1)}, u32[]{:S(2)}) copy-start(f32[512]{0:T(512)S(1)} %get-tuple-element.589) | copy-start | bytes 6148
  12.1 372.5 %copy-start.94 = (f32[512]{0:T(512)}, f32[512]{0:T(512)S(1)}, u32[]{:S(2)}) copy-start(f32[512]{0:T(512)S(1)} %fusion.176) | copy-start | bytes 6148
  74.0 503.2 %all-gather.23.cloned.1.call-start = ((), (), s32[]{:S(2)}) async-start(), calls=%async_computation.17 | async-start | bytes 5242880 | tf_op jit(solution)/shard_map/all_gather | solution.py:141
  74.0 317.8 %copy-start.60 = (f32[512]{0:T(512)}, f32[512]{0:T(512)S(1)}, u32[]{:S(2)}) copy-start(f32[512]{0:T(512)S(1)} %fusion.180) | copy-start | bytes 6148
  78.0 615.7 %all-gather.17.cloned.1.call-start = ((), (), s32[]{:S(2)}) async-start(), calls=%async_computation.14 | async-start | bytes 2162688 | tf_op jit(solution)/shard_map/all_gather | solution.py:132
  78.5 625.0 %all-gather.19.cloned.1.call-start = ((), (), s32[]{:S(2)}) async-start(), calls=%async_computation.15 | async-start | bytes 8650752 | tf_op jit(solution)/shard_map/all_gather | solution.py:166
  79.3 682.5 %all-gather.21.cloned.1.call-start = ((), (), s32[]{:S(2)}) async-start(), calls=%async_computation.16 | async-start | bytes 8650752 | tf_op jit(solution)/shard_map/all_gather | solution.py:167
  131.3 27.5 collective-permute-start
  134.9 46.3 %collective-permute-start.2 = (bf16[512,1024]{1,0:T(8,128)(2,1)S(1)}, bf16[512,1024]{1,0:T(8,128)(2,1)}, u32[]{:S(2)}, u32[]{:S(2)}) collective-permute-start(bf16[512,1024]{1,0:T(8,128)(2,1)S(1)} %add_convert_fusion.10), channel_id=1, source_target_pairs={{0,3},{1,0},{2,1},{3,2},{4,7},{5,4},{6,5},{7,6},{8,11},{9,8},{10,9... | collective-permute-start | bytes 3145736 | tf_op jit(solution)/shard_map/ppermute | solution.py:15
  160.4 238.8 %collective-permute-start.1 = (bf16[1024,1024]{1,0:T(8,128)(2,1)}, bf16[1024,1024]{1,0:T(8,128)(2,1)}, u32[]{:S(2)}, u32[]{:S(2)}) collective-permute-start(bf16[1024,1024]{1,0:T(8,128)(2,1)} %pad_maximum_fusion), channel_id=1, source_target_pairs={{0,2},{1,3},{2,0},{3,1},{4,6},{5,7},{6,4},{7,5},{8,10},{9,11},{10,... | collective-permute-start | bytes 6291464 | tf_op jit(solution)/shard_map/ppermute | solution.py:15
  161.1 1104.6 %reduce-scatter.15.cloned.1.call-start = ((), (), s32[]{:S(2)}) async-start(), calls=%async_computation.20 | async-start | bytes 5242880 | tf_op jit(solution)/shard_map/reduce_scatter | solution.py:225
  163.5 221.1 %copy-start.135 = (f32[1024]{0:T(1024)S(1)}, f32[1024]{0:T(1024)}, u32[]{:S(2)}) copy-start(f32[1024]{0:T(1024)} %param.44) | copy-start | bytes 12292
  183.8 241.2 %collective-permute-start.3 = (bf16[1024,1024]{1,0:T(8,128)(2,1)}, bf16[1024,1024]{1,0:T(8,128)(2,1)}, u32[]{:S(2)}, u32[]{:S(2)}) collective-permute-start(bf16[1024,1024]{1,0:T(8,128)(2,1)} %pad_maximum_fusion.1), channel_id=1, source_target_pairs={{0,2},{1,3},{2,0},{3,1},{4,6},{5,7},{6,4},{7,5},{8,10},{9,11},{10,... | collective-permute-start | bytes 6291464 | tf_op jit(solution)/shard_map/ppermute | solution.py:15
  593.6 96.1 %copy-start.125 = (f32[16]{0:T(128)S(1)}, f32[16]{0:T(128)}, u32[]{:S(2)}) copy-start(f32[16]{0:T(128)} %param.46) | copy-start | bytes 196
  701.9 148.9 %copy-start.100 = (f32[512]{0:T(512)}, f32[512]{0:T(512)S(1)}, u32[]{:S(2)}) copy-start(f32[512]{0:T(512)S(1)} %broadcast_multiply_fusion.5) | copy-start | bytes 6148
  703.5 147.3 %copy-start.120 = (f32[512]{0:T(512)}, f32[512]{0:T(512)S(1)}, u32[]{:S(2)}) copy-start(f32[512]{0:T(512)S(1)} %fusion.178) | copy-start | bytes 6148
  1049.0 258.4 %reduce-scatter.11.cloned.1.call-start = ((), (), s32[]{:S(2)}) async-start(), calls=%async_computation.18 | async-start | bytes 5242880 | tf_op jit(solution)/shard_map/reduce_scatter | solution.py:225
  1232.9 154.2 %reduce-scatter.17.cloned.1.call-start = ((), (), s32[]{:S(2)}) async-start(), calls=%async_computation.21 | async-start | bytes 5242880 | tf_op jit(solution)/shard_map/reduce_scatter | solution.py:228
  1233.6 233.0 %reduce-scatter.13.cloned.1.call-start = ((), (), s32[]{:S(2)}) async-start(), calls=%async_computation.19 | async-start | bytes 5242880 | tf_op jit(solution)/shard_map/reduce_scatter | solution.py:228
  1234.2 384.9 %reduce-scatter.19.cloned.1.call-start = ((), (), s32[]{:S(2)}) async-start(), calls=%async_computation.22 | async-start | bytes 4325376 | tf_op jit(solution)/shard_map/reduce_scatter | solution.py:268
  1241.6 528.3 %reduce-scatter.25.cloned.1.call-start = ((), (), s32[]{:S(2)}) async-start(), calls=%async_computation.25 | async-start | bytes 4325376 | tf_op jit(solution)/shard_map/reduce_scatter | solution.py:271
  1248.3 662.9 %all-reduce.3.cloned.1.call-start = ((), (), s32[]{:S(2)}) async-start(), calls=%async_computation.28 | async-start | bytes 181248 | tf_op jit(solution)/shard_map/psum | solution.py:275
  1392.9 79.8 %copy-start.103 = (f32[512]{0:T(512)S(1)}, f32[512]{0:T(512)}, u32[]{:S(2)}) copy-start(f32[512]{0:T(512)} %copy-done.102) | copy-start | bytes 6148
  1477.3 587.0 %reduce-scatter.21.cloned.1.call-start = ((), (), s32[]{:S(2)}) async-start(), calls=%async_computation.23 | async-start | bytes 4325376 | tf_op jit(solution)/shard_map/reduce_scatter | solution.py:269
  1483.9 730.7 %reduce-scatter.23.cloned.1.call-start = ((), (), s32[]{:S(2)}) async-start(), calls=%async_computation.24 | async-start | bytes 4325376 | tf_op jit(solution)/shard_map/reduce_scatter | solution.py:270
  1490.3 1086.4 %reduce-scatter.27.cloned.1.call-start = ((), (), s32[]{:S(2)}) async-start(), calls=%async_computation.26 | async-start | bytes 17301504 | tf_op jit(solution)/shard_map/reduce_scatter | solution.py:272
  1516.3 1425.3 %reduce-scatter.29.cloned.1.call-start = ((), (), s32[]{:S(2)}) async-start(), calls=%async_computation.27 | async-start | bytes 17301504 | tf_op jit(solution)/shard_map/reduce_scatter | solution.py:273
  (130 other events, 1181.6 us)
Sparse Core Ops, SparseCore 0:
  10.9 59.0 all-gather.10
  73.0 55.1 all-gather.14
  131.2 253.4 all-gather.8
  386.1 79.5 all-gather.12
  467.1 79.2 all-gather.22
  549.2 54.9 all-gather.16
  607.1 75.9 all-gather.18
  686.0 75.7 all-gather.20
  1049.1 75.4 reduce-scatter.14
  1232.1 75.3 reduce-scatter.10
  1309.8 77.3 reduce-scatter.16
  1389.3 77.2 reduce-scatter.12
  1469.5 149.5 reduce-scatter.18
  1621.8 148.0 reduce-scatter.24
  1777.3 133.8 all-reduce.2
  1913.9 150.3 reduce-scatter.20
  2066.9 147.6 reduce-scatter.22
  2217.3 359.3 reduce-scatter.26
  2579.6 361.9 reduce-scatter.28
